TPU v7x, 32 devices: a whole 2x2x4 slice. The times are simulated.
32 devices in a mesh: blk: 2 (over y), visit: 4 (over z), patch: 2 (over x), row: 2 (over core).
Axes of the slice: x: 2, y: 2, z: 4, core: 2. Of those that a mesh axis runs over, the one named last changes fastest.
Arguments:
- exposures: bfloat16 [8, 4, 256, 4096], P(('blk', 'visit'), 'patch', 'row'), parts along dimension 0, may hold values from -6 to 6
- kernel_choice: int32 [8, 4], P(('blk', 'visit'), 'patch'), parts along dimension 0, may hold values from 0 to 15
- kernel_coeffs: float32 [9, 16], replicated, may hold values from -2 to 2
- row_taps: bfloat16 [9, 21], replicated, may hold values from -1.25 to 1.25
- column_taps: bfloat16 [9, 21], replicated, may hold values from -1.25 to 1.25
- visit_weight: bfloat16 [8, 4], P('blk'), parts along dimension 0, may hold values from 0.29882812 to 3
- footprints: int32 [3, 8, 2, 32], P(None, 'blk', 'patch'), parts along dimension 1, may hold values from -1 to 3967, as said below
- star_coeffs: float32 [4, 32, 2048], P(('blk', 'patch'), None, ('visit', 'row')), parts along dimension 0, may hold values from -180 to 180
Outputs:
- coadd: float32 [4, 8, 256, 128], P(('blk', 'patch'), 'visit', 'row'), parts along dimension 0
- psf_factor: float32 [4, 32, 32], P(('blk', 'patch')), parts along dimension 0
- whitened: float32 [4, 32, 2048], P(('blk', 'patch'), None, ('visit', 'row')), parts along dimension 0
There are 2 independent parts, one for each index of `blk`. A program takes and returns all parts, laid end to end along the dimension named above; an argument that names none is the same for every part. Nothing has to cross between parts.
Inputs may be any that keep to these rules, and one draw needn't show every extreme that they name: `footprints`: for source visit index s, patch p and entry q: field 0 is the source block k of visit s + k // 2 and CCD p * 2 + k % 2, or -1 for an empty entry; field 1 is the column offset, at most 3967; field 2 the tile slot, 0 to 1. Entry q goes to the owner with visit index q // 8, so at most 8 entries pass from one source to one owner, and in every patch one owner receives 8 live entries from every source. Every tile slot of every owner receives at least one live entry. Empty entries hold 0 in fields 1 and 2.
All inputs are finite; a program needn't handle non-finite values.
Results may differ from a plain program's by a relative error of at most 0.007.
Values may be sent and summed in bfloat16 or wider, within the bound.
A program may use at most 192 MiB of HBM per device.

v0:
```python
import functools
import math

import jax
import jax.numpy as jnp
from jax import lax
from jax.sharding import PartitionSpec as P

NBASIS = 9
NCOEF = 16
V_DEV = 1
C_DEV = 2
R_DEV = 128
CW = 4096
TW = 128
CAP = 8
TILES_DEV = 2
HALF = 10
SLABS = 2


HIGHEST = lax.Precision.HIGHEST
BILINEAR = (0.28125, 0.46875, 0.09375, 0.15625)


def combined_all(part, axis, combine):
    gathered = lax.all_gather(part, axis)

    def take(source):
        return lax.dynamic_index_in_dim(gathered, source, 0, False)

    return lax.fori_loop(
        1, lax.axis_size(axis), lambda source, state: combine(state, take(source)), take(0)
    )


def extended_2(cells, sides, width):
    for axis, dim in sides:
        count = lax.axis_size(axis)
        ends = count - 1
        head = lax.slice_in_dim(cells, 0, width, axis=dim)
        tail = lax.slice_in_dim(cells, cells.shape[dim] - width, cells.shape[dim], axis=dim)
        cells = jnp.concatenate(
            [
                lax.ppermute(tail, axis, [(i, (i + 1) % count) for i in range(ends)]),
                cells,
                lax.ppermute(head, axis, [((i + 1) % count, i) for i in range(ends)]),
            ],
            axis=dim,
        )
    return cells


def band_matrix(taps, width):
    basis_count, tap_count = taps.shape
    span = width + tap_count - 1
    offsets = jnp.arange(span)[:, None] - jnp.arange(width)[None, :]
    picks = (offsets[None, :, :] == jnp.arange(tap_count)[:, None, None]).astype(jnp.float32)
    banded = jnp.einsum("bt,tuw->ubw", taps.astype(jnp.float32), picks, precision=HIGHEST)
    return banded.reshape(span, basis_count * width).astype(jnp.bfloat16)


def row_matrix(mixing, out_rows):
    basis_count, tap_count = mixing.shape
    extended = out_rows + tap_count
    offsets = jnp.arange(extended)[None, :] - jnp.arange(out_rows)[:, None] - 1
    picks = (offsets[None, :, :] == jnp.arange(tap_count)[:, None, None]).astype(jnp.float32)
    return jnp.einsum("bt,tie->ieb", mixing.astype(jnp.float32), picks, precision=HIGHEST).astype(
        jnp.bfloat16
    )


def entry_weights(table, slab_ids, source_ids, patch_index):
    safe_ids = jnp.maximum(slab_ids, 0)
    visit_ids = source_ids * V_DEV + safe_ids // C_DEV
    ccd_ids = patch_index * C_DEV + safe_ids % C_DEV
    flat_ids = visit_ids * table.shape[1] + ccd_ids
    matches = flat_ids[..., None] == jnp.arange(table.size, dtype=jnp.int32)
    picked = jnp.sum(jnp.where(matches, table.reshape(-1).astype(jnp.float32), 0.0), axis=-1)
    return jnp.where(slab_ids >= 0, picked, 0.0)


def on_device(
    exposures,
    kernel_choice,
    kernel_coeffs,
    row_taps,
    column_taps,
    visit_weight,
    footprints,
    star_coeffs,
):
    local_stars = star_coeffs[0]
    gram = jnp.dot(
        local_stars, local_stars.T, precision=HIGHEST, preferred_element_type=jnp.float32
    )
    star_total = local_stars.shape[1] * lax.axis_size("visit") * lax.axis_size("row")

    def combine_factors(first, second):
        joined = jnp.dot(first, first.T, precision=HIGHEST) + jnp.dot(
            second, second.T, precision=HIGHEST
        )
        return jnp.linalg.cholesky(joined)

    lower = combined_all(jnp.linalg.cholesky(gram), ("visit", "row"), combine_factors)
    factor = lower / math.sqrt(star_total)
    whitened = lax.linalg.triangular_solve(factor, local_stars, left_side=True, lower=True)
    factor_diag = jnp.diagonal(factor)[:NBASIS]
    basis_scale = factor_diag / jnp.sqrt(jnp.mean(factor_diag * factor_diag))
    images = exposures.reshape(SLABS, R_DEV, CW)
    extended = extended_2(images, (("row", 1),), HALF + 1)
    ext_rows = R_DEV + 2 * HALF + 2
    out_rows = R_DEV + 1
    choice_ids = kernel_choice.reshape(SLABS)
    matches = choice_ids[:, None] == jnp.arange(NCOEF, dtype=jnp.int32)[None, :]
    coefficient = (
        jnp.sum(jnp.where(matches[:, None, :], kernel_coeffs[None, :, :], 0.0), axis=-1)
        * basis_scale[None, :]
    )
    mixing = (coefficient[:, :, None] * row_taps.astype(jnp.float32)[None]).astype(jnp.bfloat16)
    row_mats = jax.vmap(functools.partial(row_matrix, out_rows=out_rows))(mixing)
    banded = band_matrix(column_taps, TW)
    left_band = banded[:HALF]
    middle = banded[HALF : HALF + TW]
    right_band = banded[HALF + TW :]
    blocks = CW // TW

    def match_slab(operands):
        slab_rows, row_mat = operands
        by_block = slab_rows.reshape(ext_rows, blocks, TW)
        leading = jnp.pad(by_block[:, :-1, TW - HALF :], ((0, 0), (1, 0), (0, 0)))
        trailing = jnp.pad(by_block[:, 1:, :HALF], ((0, 0), (0, 1), (0, 0)))
        filtered = (
            jnp.dot(by_block, middle, preferred_element_type=jnp.float32)
            + jnp.dot(leading, left_band, preferred_element_type=jnp.float32)
            + jnp.dot(trailing, right_band, preferred_element_type=jnp.float32)
        )
        filtered = filtered.astype(jnp.bfloat16).reshape(ext_rows, blocks, NBASIS, TW)
        summed = jnp.einsum("ieb,ekbw->ikw", row_mat, filtered, preferred_element_type=jnp.float32)
        return summed.astype(jnp.bfloat16).reshape(out_rows, CW)

    matched = lax.map(match_slab, (extended, row_mats))
    last_core = lax.axis_index("row") == lax.axis_size("row") - 1
    inside = (jnp.arange(out_rows) < R_DEV) | jnp.logical_not(last_core)
    matched = jnp.where(inside[None, :, None], matched, jnp.zeros_like(matched))
    source_index = lax.axis_index("visit")
    patch_index = lax.axis_index("patch")
    sources = footprints.shape[1]
    own_list = footprints[:, :, 0, :]
    entries = lax.dynamic_index_in_dim(own_list, source_index, axis=1, keepdims=False)
    slab_ids = entries[0]

    def cut_window(slab_id, offset):
        start = (jnp.maximum(slab_id, 0), jnp.int32(0), offset)
        return lax.dynamic_slice(matched, start, (1, out_rows, TW + 1))[0]

    cut = jax.vmap(cut_window)(slab_ids, entries[1])
    warped = (
        BILINEAR[0] * cut[:, :-1, :-1].astype(jnp.float32)
        + BILINEAR[1] * cut[:, :-1, 1:].astype(jnp.float32)
        + BILINEAR[2] * cut[:, 1:, :-1].astype(jnp.float32)
        + BILINEAR[3] * cut[:, 1:, 1:].astype(jnp.float32)
    ).astype(jnp.bfloat16)
    incoming = lax.dynamic_slice_in_dim(own_list, source_index * CAP, CAP, axis=2)
    in_weight = entry_weights(
        visit_weight, incoming[0], jnp.arange(sources, dtype=jnp.int32)[:, None], patch_index
    )
    tile_ids = jnp.arange(TILES_DEV, dtype=jnp.int32)[:, None, None]
    spread = jnp.where(incoming[2][None] == tile_ids, in_weight[None], 0.0)
    totals = jnp.sum(spread, axis=(1, 2))
    flat_size = R_DEV * TW
    outgoing = warped.reshape(sources, CAP, R_DEV, TW)
    received = lax.all_to_all(outgoing, "visit", split_axis=0, concat_axis=0, tiled=True)
    partials = jnp.einsum(
        "gsq,sqf->sgf",
        spread.astype(jnp.bfloat16),
        received.reshape(sources, CAP, flat_size),
        preferred_element_type=jnp.float32,
    )
    partials = partials.astype(jnp.bfloat16).astype(jnp.float32)
    numerator = jnp.sum(partials, axis=0).reshape(TILES_DEV, R_DEV, TW)
    coadd = (numerator / totals[:, None, None])[None]
    return (coadd, factor[None], whitened[None])


def solution(mesh):
    in_specs = (
        P(("blk", "visit"), "patch", "row", None),
        P(("blk", "visit"), "patch"),
        P(),
        P(),
        P(),
        P("blk", None),
        P(None, "blk", "patch", None),
        P(("blk", "patch"), None, ("visit", "row")),
    )
    out_specs = (
        P(("blk", "patch"), "visit", "row", None),
        P(("blk", "patch"), None, None),
        P(("blk", "patch"), None, ("visit", "row")),
    )
    return jax.shard_map(
        on_device, mesh=mesh, in_specs=in_specs, out_specs=out_specs, check_vma=False
    )
```

profile of v0, /device:TPU:0, one launch (start us, length us, event | category | flops | bytes accessed | tf_op | source)
XLA Modules:
  0.0 304.9 jit_solution(12800378180615243677)
XLA Ops:
  0.7 1.9 fusion.64
  2.5 1.3 collective-permute-start.1
  3.8 3.7 %collective-permute-start = (bf16[2,11,4096]{2,1,0:T(8,128)(2,1)}, bf16[2,11,4096]{2,1,0:T(8,128)(2,1)}, u32[]{:S(2)}, u32[]{:S(2)}) collective-permute-start(bf16[2,11,4096]{2,1,0:T(8,128)(2,1)} %get-tuple-element.233), channel_id=1, source_target_pairs={{0,1},{2,3},{4,5},{6,7},{8,9},{10,11},{12,13},{14,15},{16,17},{18,... | collective-permute-start | bytes 540680 | tf_op jit(solution)/shard_map/ppermute | solution.py:45
  7.6 0.7 convert_element_type.75
  8.3 0.7 iota_compare_fusion.12
  9.0 0.8 select_reduce_fusion.3
  10.1 2.9 cholesky.55
  13.1 0.6 compare_reduce_fusion.1
  13.7 0.6 select_select_fusion.1
  14.4 15.7 %all-gather = f32[256,32]{1,0:T(8,128)S(1)} all-gather(f32[32,32]{1,0:T(8,128)S(1)} %select_select_fusion.1), channel_id=2, replica_groups=mesh['blk'=2,'visit'=4,'patch'=2,'row'=2] {'visit','row'}, dimensions={0}, use_global_device_ids=true | all-gather | bytes 36864 | tf_op jit(solution)/shard_map/all_gather | solution.py:27
  30.1 32.7 %while.27 = (s32[]{:T(128)}, f32[32,32]{1,0:T(8,128)S(1)}, f32[8,32,32]{2,1,0:T(8,128)S(1)}, s32[]{:T(128)}, s32[]{:T(128)}, /*index=5*/s32[]{:T(128)}) while((s32[]{:T(128)}, f32[32,32]{1,0:T(8,128)S(1)}, f32[8,32,32]{2,1,0:T(8,128)S(1)}, s32[]{:T(128)}, s32[]{:T(128)}, /*index=5*/s32[]{:T(128)}) %tuple.85), condition=%wide.region_5.7_spmd, body=%wide.region_4.6_spmd.sunk | while | flops 795684 | bytes 78197 | solution.py:32
  30.5 2.9 cholesky.118
  33.5 0.6 compare_reduce_fusion.3
  34.1 0.6 select_select_fusion.3
  35.2 2.9 cholesky.118
  38.1 0.6 compare_reduce_fusion.3
  38.8 0.6 select_select_fusion.3
  39.9 2.9 cholesky.118
  42.8 0.6 compare_reduce_fusion.3
  43.5 0.6 select_select_fusion.3
  44.5 2.9 cholesky.118
  47.5 0.6 compare_reduce_fusion.3
  48.1 0.6 select_select_fusion.3
  49.2 2.9 cholesky.118
  52.2 0.6 compare_reduce_fusion.3
  52.8 0.6 select_select_fusion.3
  53.9 2.9 cholesky.118
  56.8 0.6 compare_reduce_fusion.3
  57.5 0.6 select_select_fusion.3
  58.6 2.9 cholesky.118
  61.5 0.6 compare_reduce_fusion.3
  62.2 0.6 select_select_fusion.3
  63.5 1.3 fusion.60
  64.7 0.7 gather_fusion
  67.2 0.8 convert_bitcast_fusion
  68.7 1.8 copy.62
  71.7 3.7 %pad_maximum_fusion = bf16[2,150,4096]{2,1,0:T(8,128)(2,1)} fusion(bf16[2,11,4096]{2,1,0:T(8,128)(2,1)S(1)} %collective-permute-done.1, bf16[2,128,4096]{2,1,0:T(8,128)(2,1)} %bitcast.132, bf16[2,11,4096]{2,1,0:T(8,128)(2,1)} %collective-permute-done), kind=kLoop, calls=%fused_computation.38 | loop fusion | flops 7372800 | bytes 4915200 | tf_op jit(solution)/shard_map/concatenate | solution.py:43
  75.4 168.9 %while.28 = (s32[]{:T(128)}, bf16[2,129,4096]{2,1,0:T(8,128)(2,1)}, bf16[2,129,150,9]{2,1,3,0:T(8,128)(2,1)}, bf16[2,150,4096]{2,1,0:T(8,128)(2,1)}, bf16[128,11...) while((s32[]{:T(128)}, bf16[2,129,4096]{2,1,0:T(8,128)(2,1)}, ...), condition=%wide.region_8.10_spmd, body=%wide.region_7.9_spmd.sunk | while | flops 3080515584 | bytes 156469280 | solution.py:142
  75.4 1.4 constant_dynamic-slice_fusion.6
  77.0 9.1 %fusion.98 = f32[150,32,1152]{2,1,0:T(8,128)} fusion(bf16[128,1152]{1,0:T(8,128)(2,1)S(1)} %get-tuple-element.351, bf16[152,32,128]{2,1,0:T(8,128)(2,1)S(1)} %bitcast.128), kind=kOutput, calls=%fused_computation.22.clone.1 | convolution fusion | flops 1415577600 | bytes 23642112 | tf_op jit(solution)/shard_map/while/body/eval_jaxpr/dot_general | solution.py:134
  86.1 0.9 fusion.99
  87.0 9.1 %fusion.100 = f32[150,32,1152]{2,1,0:T(8,128)} fusion(bf16[150,31,10]{2,1,0:T(8,128)(2,1)S(1)} %get-tuple-element.311, bf16[10,1152]{1,0:T(8,128)(2,1)S(1)} %get-tuple-element.352), kind=kOutput, calls=%fused_computation.18.clone.1 | convolution fusion | flops 110592000 | bytes 22234440 | tf_op jit(solution)/shard_map/while/body/eval_jaxpr/dot_general | solution.py:135
  96.1 19.5 %add_convert_fusion.3 = bf16[150,32,1152]{2,1,0:T(8,128)(2,1)} fusion(f32[150,32,1152]{2,1,0:T(8,128)} %fusion.98, f32[150,32,1152]{2,1,0:T(8,128)} %fusion.100, bf16[150,31,10]{2,1,0:T(8,128)(2,1)S(1)} %get-tuple-element.312, bf16[10,1152]{1,0:T(8,128)(2,1)S(1)} %get-tuple-element.353), kind=kOutput, calls=%fused_computation.13.clone.1 | convolution fusion | flops 127180800 | bytes 55412040 | tf_op jit(solution)/shard_map/while/body/eval_jaxpr/dot_general | solution.py:136
  115.6 22.9 %reshape.261 = bf16[150,32,9,128]{3,2,1,0:T(8,128)(2,1)} reshape(bf16[150,32,1152]{2,1,0:T(8,128)(2,1)} %add_convert_fusion.3) | data formatting | bytes 22118400 | tf_op jit(solution)/shard_map/while/body/eval_jaxpr/reshape | solution.py:138
  138.5 19.6 %bitcast_convert_fusion.2 = bf16[129,32,128]{2,0,1:T(8,128)(2,1)S(1)} fusion(bf16[150,32,9,128]{3,2,1,0:T(8,128)(2,1)} %reshape.261, bf16[2,129,150,9]{2,1,3,0:T(8,128)(2,1)} %get-tuple-element.349, s32[]{:T(128)S(6)} %copy.102), kind=kOutput, calls=%fused_computation.16.clone.1 | convolution fusion | flops 1427165184 | bytes 21344260 | tf_op jit(solution)/shard_map/while/body/eval_jaxpr/ieb,ekbw->ikw/dot_general | solution.py:139
  158.7 1.1 constant_dynamic-update-slice_fusion.2
  159.8 1.4 constant_dynamic-slice_fusion.6
  161.5 9.1 %fusion.98 = f32[150,32,1152]{2,1,0:T(8,128)} fusion(bf16[128,1152]{1,0:T(8,128)(2,1)S(1)} %get-tuple-element.351, bf16[152,32,128]{2,1,0:T(8,128)(2,1)S(1)} %bitcast.128), kind=kOutput, calls=%fused_computation.22.clone.1 | convolution fusion | flops 1415577600 | bytes 23642112 | tf_op jit(solution)/shard_map/while/body/eval_jaxpr/dot_general | solution.py:134
  170.5 0.9 fusion.99
  171.5 9.1 %fusion.100 = f32[150,32,1152]{2,1,0:T(8,128)} fusion(bf16[150,31,10]{2,1,0:T(8,128)(2,1)S(1)} %get-tuple-element.311, bf16[10,1152]{1,0:T(8,128)(2,1)S(1)} %get-tuple-element.352), kind=kOutput, calls=%fused_computation.18.clone.1 | convolution fusion | flops 110592000 | bytes 22234440 | tf_op jit(solution)/shard_map/while/body/eval_jaxpr/dot_general | solution.py:135
  180.6 19.5 %add_convert_fusion.3 = bf16[150,32,1152]{2,1,0:T(8,128)(2,1)} fusion(f32[150,32,1152]{2,1,0:T(8,128)} %fusion.98, f32[150,32,1152]{2,1,0:T(8,128)} %fusion.100, bf16[150,31,10]{2,1,0:T(8,128)(2,1)S(1)} %get-tuple-element.312, bf16[10,1152]{1,0:T(8,128)(2,1)S(1)} %get-tuple-element.353), kind=kOutput, calls=%fused_computation.13.clone.1 | convolution fusion | flops 127180800 | bytes 55412040 | tf_op jit(solution)/shard_map/while/body/eval_jaxpr/dot_general | solution.py:136
  200.1 22.9 %reshape.261 = bf16[150,32,9,128]{3,2,1,0:T(8,128)(2,1)} reshape(bf16[150,32,1152]{2,1,0:T(8,128)(2,1)} %add_convert_fusion.3) | data formatting | bytes 22118400 | tf_op jit(solution)/shard_map/while/body/eval_jaxpr/reshape | solution.py:138
  223.0 19.6 %bitcast_convert_fusion.2 = bf16[129,32,128]{2,0,1:T(8,128)(2,1)S(1)} fusion(bf16[150,32,9,128]{3,2,1,0:T(8,128)(2,1)} %reshape.261, bf16[2,129,150,9]{2,1,3,0:T(8,128)(2,1)} %get-tuple-element.349, s32[]{:T(128)S(6)} %copy.102), kind=kOutput, calls=%fused_computation.16.clone.1 | convolution fusion | flops 1427165184 | bytes 21344260 | tf_op jit(solution)/shard_map/while/body/eval_jaxpr/ieb,ekbw->ikw/dot_general | solution.py:139
  243.2 1.1 constant_dynamic-update-slice_fusion.2
  244.3 10.8 %copy.64 = bf16[2,129,4096]{1,0,2:T(2,128)(2,1)} copy(bf16[2,129,4096]{2,1,0:T(8,128)(2,1)} %get-tuple-element.182) | data formatting | bytes 4227072 | tf_op jit(solution)/shard_map/while | solution.py:142
  255.1 8.0 %broadcast_select_fusion = bf16[2,129,4096]{1,0,2:T(2,128)(2,1)} fusion(bf16[2,129,4096]{1,0,2:T(2,128)(2,1)} %copy.64, pred[129]{0:T(512)(128)(4,1)S(1)} %copy-done.6), kind=kLoop, calls=%fused_computation.34 | loop fusion | flops 1056768 | bytes 4227201 | tf_op jit(solution)/shard_map/jit(_where)/select_n | solution.py:145
  263.0 6.2 %gather_fusion.1 = bf16[32,129,129]{1,0,2:T(8,128)(2,1)S(1)} fusion(bf16[2,129,4096]{1,0,2:T(2,128)(2,1)} %broadcast_select_fusion, s32[32]{0:T(128)S(1)} %copy-done.1), kind=kCustom, calls=%fused_computation.1 | custom fusion | bytes 2130432 | tf_op jit(solution)/shard_map/vmap()/gather | solution.py:155
  269.3 1.0 fusion.32
  270.3 2.0 copy.65
  272.3 5.2 %all-to-all-start = ((bf16[4,8,128,128]{3,1,2,0:T(8,128)(2,1)}), bf16[4,8,128,128]{3,1,2,0:T(8,128)(2,1)S(1)}, u32[]{:S(2)}, u32[]{:S(2)}) async-start(bf16[4,8,128,128]{3,1,2,0:T(8,128)(2,1)} %copy.65), calls=%async_computation | async-start | bytes 2097152 | tf_op jit(solution)/shard_map/all_to_all | solution.py:173
  277.6 3.2 %custom-call.5 = f32[1,32,32]{1,2,0:T(8,128)S(1)} custom-call(f32[1,32,32]{2,1,0:T(8,128)} %get-tuple-element.237), custom_call_target="InvertDiagBlocksLowerTriangular" | custom-call | tf_op jit(solution)/shard_map/triangular_solve | solution.py:107
  281.2 0.8 convolution_bitcast_fusion
  282.1 21.6 %all-to-all-done = bf16[4,8,128,128]{3,1,2,0:T(8,128)(2,1)S(1)} async-done(((bf16[4,8,128,128]{3,1,2,0:T(8,128)(2,1)}), bf16[4,8,128,128]{3,1,2,0:T(8,128)(2,1)S(1)}, u32[]{:S(2)}, u32[]{:S(2)}) %all-to-all-start) | async-done | bytes 1048608 | tf_op jit(solution)/shard_map/all_to_all | solution.py:173
  304.2 0.7 bitcast_divide_fusion
  (90 shorter events, 9.5 us)
Async XLA Ops:
  0.6 9.3 %copy-start = (f32[1,32,256]{2,1,0:T(8,128)S(1)}, f32[1,32,256]{2,1,0:T(8,128)}, u32[]{:S(2)}) copy-start(f32[1,32,256]{2,1,0:T(8,128)} %param.20) | copy-start | bytes 98308
  0.6 66.1 %copy-start.5 = (bf16[9,21]{1,0:T(8,128)(2,1)S(1)}, bf16[9,21]{1,0:T(8,128)(2,1)}, u32[]{:S(2)}) copy-start(bf16[9,21]{1,0:T(8,128)(2,1)} %param.17) | copy-start | bytes 1138
  2.5 69.2 %collective-permute-start.1 = (bf16[2,11,4096]{2,1,0:T(8,128)(2,1)}, bf16[2,11,4096]{2,1,0:T(8,128)(2,1)S(1)}, u32[]{:S(2)}, u32[]{:S(2)}) collective-permute-start(bf16[2,11,4096]{2,1,0:T(8,128)(2,1)} %get-tuple-element.234), channel_id=1, source_target_pairs={{1,0},{3,2},{5,4},{7,6},{9,8},{11,10},{13,12},{15,14},{17,16},{19,... | collective-permute-start | bytes 540680 | tf_op jit(solution)/shard_map/ppermute | solution.py:47
  3.8 67.9 %collective-permute-start = (bf16[2,11,4096]{2,1,0:T(8,128)(2,1)}, bf16[2,11,4096]{2,1,0:T(8,128)(2,1)}, u32[]{:S(2)}, u32[]{:S(2)}) collective-permute-start(bf16[2,11,4096]{2,1,0:T(8,128)(2,1)} %get-tuple-element.233), channel_id=1, source_target_pairs={{0,1},{2,3},{4,5},{6,7},{8,9},{10,11},{12,13},{14,15},{16,17},{18,... | collective-permute-start | bytes 540680 | tf_op jit(solution)/shard_map/ppermute | solution.py:45
  68.7 2.4 copy-start.3
  68.7 2.4 copy-start.2
  244.3 10.8 %copy-start.6 = (pred[129]{0:T(512)(128)(4,1)S(1)}, pred[129]{0:T(512)(128)(4,1)}, u32[]{:S(2)}) copy-start(pred[129]{0:T(512)(128)(4,1)} %compare_or_fusion) | copy-start | bytes 391
  255.1 8.0 %copy-start.1 = (s32[32]{0:T(128)S(1)}, s32[32]{0:T(128)}, u32[]{:S(2)}) copy-start(s32[32]{0:T(128)} %get-tuple-element.245) | copy-start | bytes 388
  270.3 7.2 %copy-start.7 = (bf16[4,4]{1,0:T(4,128)(2,1)S(1)}, bf16[4,4]{1,0:T(4,128)(2,1)}, u32[]{:S(2)}) copy-start(bf16[4,4]{1,0:T(4,128)(2,1)} %param.18) | copy-start | bytes 100
  270.3 10.4 %copy-start.4 = (s32[3,4,1,32]{3,2,1,0:T(1,128)S(1)}, s32[3,4,1,32]{3,2,1,0:T(1,128)}, u32[]{:S(2)}) copy-start(s32[3,4,1,32]{3,2,1,0:T(1,128)} %param.19) | copy-start | bytes 4612
  272.3 31.4 %all-to-all-start = ((bf16[4,8,128,128]{3,1,2,0:T(8,128)(2,1)}), bf16[4,8,128,128]{3,1,2,0:T(8,128)(2,1)S(1)}, u32[]{:S(2)}, u32[]{:S(2)}) async-start(bf16[4,8,128,128]{3,1,2,0:T(8,128)(2,1)} %copy.65), calls=%async_computation | async-start | bytes 2097152 | tf_op jit(solution)/shard_map/all_to_all | solution.py:173
where the time goes:
time: 307 us; the launch traced here: 305 us
  matrix products  119 us (39%)
  local copies, waits for them, and re-layouts  79.8 us (26%)
  other arithmetic  56.3 us (18%)
  waiting for transfers between devices  21.7 us (7%)
  blocking collectives  15.7 us (5%)
  starting transfers between devices  10.2 us (3%)
    reshape x2, local copies, waits for them, and re-layouts, match_slab(): filtered.astype(jnp.bfloat16).reshape(ext_rows, blocks, NBASIS, TW)  45.8 us
    dot_general x2, matrix products, match_slab(): jnp.einsum('ieb,ekbw->ikw', row_mat, filtered, preferred_element_type=jnp...  39.2 us
    dot_general x2, matrix products, match_slab(): jnp.dot(trailing, right_band, preferred_element_type=jnp.float32)  39 us
    another operation x21, other arithmetic, combine_factors(): return jnp.linalg.cholesky(joined)  25.2 us
    all_to_all x1, waiting for transfers between devices, on_device(): lax.all_to_all(outgoing, 'visit', split_axis=0, concat_axis=0, tiled=True)  21.6 us
    dot_general x2, matrix products, match_slab(): jnp.dot(leading, left_band, preferred_element_type=jnp.float32)  18.1 us
    dot_general x2, matrix products, match_slab(): jnp.dot(by_block, middle, preferred_element_type=jnp.float32)  18.1 us
    all_gather x1, blocking collectives, combined_all(): gathered = lax.all_gather(part, axis)  15.7 us
  transfers between devices with their start and end apart: 3, of which 1 were waited for; matrix products, arithmetic and copies ran while one was open for 17% of the time, Pallas kernels for 0%

commit v1 on v0

v1 whole, which is shorter than its diff:
```python
import functools
import math

import jax
import jax.numpy as jnp
from jax import lax
from jax.experimental import pallas as pl
from jax.experimental.pallas import tpu as pltpu
from jax.sharding import PartitionSpec as P

NBASIS = 9
NTAPS = 21
C_DEV = 2
R_DEV = 128
CW = 4096
TW = 128
CAP = 8
TILES_DEV = 2
HALF = 10
SLABS = 2
HALO = 16
EXT = R_DEV + HALO
NCOMP = 32
BK = NBASIS * EXT
PAD = 128
HIGHEST = lax.Precision.HIGHEST
VMEM_LIMIT = 60 * 1024 * 1024


def blended(taps, near, far):
    zero = jnp.zeros((taps.shape[0], 1), jnp.float32)
    taps = taps.astype(jnp.float32)
    return near * jnp.concatenate([taps, zero], 1) + far * jnp.concatenate([zero, taps], 1)


def column_band(taps):
    both = blended(taps, 0.375, 0.625)
    diff = jnp.arange(2 * TW)[:, None] - jnp.arange(TW)[None, :]
    picks = (diff[None] == jnp.arange(NTAPS + 1)[:, None, None]).astype(jnp.float32)
    out = jnp.einsum("bt,tuw->ubw", both, picks, precision=HIGHEST)
    return out.reshape(2 * TW, NBASIS * TW).astype(jnp.bfloat16)


def row_band(taps, row_index):
    e = jnp.arange(EXT)
    position = jnp.where(e < R_DEV, e, jnp.where(row_index == 0, e, e - EXT))
    diff = position[None, :] - jnp.arange(R_DEV)[:, None] + HALF
    steps = jnp.arange(NTAPS)[:, None, None]
    last = (jnp.arange(R_DEV)[:, None] == R_DEV - 1) & (row_index == 1)
    picks = 0.75 * (diff[None] == steps) + jnp.where(last[None], 0.0, 0.25) * (diff[None] - 1 == steps)
    out = jnp.einsum("bt,tie->ibe", taps.astype(jnp.float32), picks, precision=HIGHEST)
    return out.reshape(R_DEV, BK)


def window_kernel(entry_ref, image_ref, halo_ref, band_ref, z_ref, padded, sums):
    slots = entry_ref.shape[1]
    groups = slots // CAP * TILES_DEV
    for k in range(SLABS):
        padded[k, :, 0:PAD] = jnp.zeros((EXT, PAD), jnp.bfloat16)
        padded[k, :, PAD + CW :] = jnp.zeros((EXT, PAD), jnp.bfloat16)
        padded[k, 0:R_DEV, PAD : PAD + CW] = image_ref[k]
        padded[k, R_DEV:EXT, PAD : PAD + CW] = halo_ref[k]
    sums[...] = jnp.zeros_like(sums)
    lane = lax.broadcasted_iota(jnp.int32, (EXT, TW), 1)

    @pl.loop(0, slots)
    def _(q):
        k = entry_ref[0, q]

        @pl.when(k >= 0)
        def _():
            start = entry_ref[1, q] + (PAD - HALF)
            tile = lax.shift_right_logical(start, 7)
            shift = start - tile * TW
            back = jnp.where(shift == 0, 0, TW - shift)
            group = (q // CAP) * TILES_DEV + entry_ref[2, q]
            parts = []
            for t in range(3):
                at = pl.multiple_of((tile + t) * TW, TW)
                part = padded[k, :, pl.ds(at, TW)].astype(jnp.float32)
                parts.append(pltpu.roll(part, back, 1))
            keep = lane < TW - shift
            slot = group * SLABS + k
            sums[slot, :, 0:TW] += jnp.where(keep, parts[0], parts[1])
            sums[slot, :, TW : 2 * TW] += jnp.where(keep, parts[1], parts[2])

    @pl.loop(0, groups)
    def _(g):
        for k in range(SLABS):
            window = sums[g * SLABS + k].astype(jnp.bfloat16)
            out = jnp.dot(window, band_ref[...], preferred_element_type=jnp.float32)
            out = out.astype(jnp.bfloat16)
            for b in range(NBASIS):
                row = (k * NBASIS + b) * EXT
                z_ref[row : row + EXT, pl.ds(pl.multiple_of(g * TW, TW), TW)] = out[
                    :, b * TW : (b + 1) * TW
                ]


def factor_steps(gram, stars):
    sub = lax.broadcasted_iota(jnp.int32, (NCOMP, 1), 0)
    lane = lax.broadcasted_iota(jnp.int32, (NCOMP, NCOMP), 1)
    lower = jnp.zeros((NCOMP, NCOMP), jnp.float32)
    for j in range(NCOMP):
        inv = 1.0 / jnp.sqrt(gram[j : j + 1, j : j + 1])
        column = gram[:, j : j + 1] * inv
        lower = jnp.where((lane == j) & (sub >= j), column, lower)
        below = jnp.where(sub > j, column, 0.0)
        solved = stars[j : j + 1, :] * inv
        gram = gram - below * (gram[j : j + 1, :] * inv)
        stars = jnp.where(sub == j, solved, stars - below * solved)
    return lower, stars


def mix_kernel(
    star_total,
    choice_ref,
    weight_ref,
    gram_ref,
    star_ref,
    coeff_ref,
    rows_ref,
    z_ref,
    partial_ref,
    factor_ref,
    white_ref,
):
    gram = gram_ref[0]
    for s in range(1, gram_ref.shape[0]):
        gram = gram + gram_ref[s]
    lower, solved = factor_steps(gram, star_ref[...])
    root = math.sqrt(star_total)
    factor = lower / root
    factor_ref[...] = factor
    white_ref[...] = solved * root
    eye = lax.broadcasted_iota(jnp.int32, (NCOMP, NCOMP), 0) == lax.broadcasted_iota(
        jnp.int32, (NCOMP, NCOMP), 1
    )
    diag = jnp.sum(jnp.where(eye, factor, 0.0), axis=1, keepdims=True)[:NBASIS]
    scale = diag / jnp.sqrt(jnp.sum(diag * diag, axis=0, keepdims=True) / NBASIS)
    column = lax.broadcasted_iota(jnp.int32, (NBASIS, BK), 1)
    first = lax.broadcasted_iota(jnp.int32, (NBASIS, BK), 0) * EXT
    spread = (column >= first) & (column < first + EXT)
    sets = lax.broadcasted_iota(jnp.int32, coeff_ref.shape, 1)
    total = None
    for k in range(SLABS):
        picked = jnp.sum(
            jnp.where(sets == choice_ref[k], coeff_ref[...], 0.0), axis=1, keepdims=True
        )
        by_row = picked * scale * weight_ref[k]
        vector = jnp.sum(jnp.where(spread, by_row, 0.0), axis=0, keepdims=True)
        mixed = (rows_ref[...] * vector).astype(jnp.bfloat16)
        term = jnp.dot(
            mixed, z_ref[k * BK : (k + 1) * BK, :], preferred_element_type=jnp.float32
        )
        total = term if total is None else total + term
    for g in range(partial_ref.shape[0]):
        partial_ref[g] = total[:, g * TW : (g + 1) * TW].astype(jnp.bfloat16)


def on_device(
    exposures,
    kernel_choice,
    kernel_coeffs,
    row_taps,
    column_taps,
    visit_weight,
    footprints,
    star_coeffs,
):
    stars = star_coeffs[0]
    row_index = lax.axis_index("row")
    source_index = lax.axis_index("visit")
    patch_index = lax.axis_index("patch")
    sources = footprints.shape[1]
    groups = sources * TILES_DEV
    star_total = stars.shape[1] * lax.axis_size("visit") * lax.axis_size("row")
    gram = jnp.dot(stars, stars.T, precision=HIGHEST, preferred_element_type=jnp.float32)
    grams = lax.all_gather(gram, ("visit", "row"))
    images = exposures.reshape(SLABS, R_DEV, CW)
    edge = jnp.where(row_index == 0, images[:, R_DEV - HALO :], images[:, :HALO])
    halo = lax.ppermute(edge, "row", [(0, 1), (1, 0)])
    own_list = footprints[:, :, 0, :]
    entries = lax.dynamic_index_in_dim(own_list, source_index, axis=1, keepdims=False)
    vmem = pl.BlockSpec(memory_space=pltpu.VMEM)
    smem = pl.BlockSpec(memory_space=pltpu.SMEM)
    z = pl.pallas_call(
        window_kernel,
        out_shape=jax.ShapeDtypeStruct((SLABS * BK, groups * TW), jnp.bfloat16),
        in_specs=[smem, vmem, vmem, vmem],
        out_specs=vmem,
        scratch_shapes=[
            pltpu.VMEM((SLABS, EXT, CW + 2 * PAD), jnp.bfloat16),
            pltpu.VMEM((groups * SLABS, EXT, 2 * TW), jnp.float32),
        ],
        compiler_params=pltpu.CompilerParams(vmem_limit_bytes=VMEM_LIMIT),
        cost_estimate=pl.CostEstimate(flops=2 * 10**9, bytes_accessed=10**7, transcendentals=0),
        name="windows",
    )(entries, images, halo, column_band(column_taps))
    table = visit_weight.astype(jnp.float32)
    own_weight = lax.dynamic_slice(
        table, (source_index, patch_index * C_DEV), (1, C_DEV)
    ).reshape(C_DEV)
    partial, factor, whitened = pl.pallas_call(
        functools.partial(mix_kernel, star_total),
        out_shape=(
            jax.ShapeDtypeStruct((groups, R_DEV, TW), jnp.bfloat16),
            jax.ShapeDtypeStruct((NCOMP, NCOMP), jnp.float32),
            jax.ShapeDtypeStruct(stars.shape, jnp.float32),
        ),
        in_specs=[smem, smem, vmem, vmem, vmem, vmem, vmem],
        out_specs=(vmem, vmem, vmem),
        compiler_params=pltpu.CompilerParams(vmem_limit_bytes=VMEM_LIMIT),
        name="mix",
    )(
        kernel_choice.reshape(SLABS),
        own_weight,
        grams,
        stars,
        kernel_coeffs,
        row_band(row_taps, row_index),
        z,
    )
    incoming = lax.dynamic_slice_in_dim(own_list, source_index * CAP, CAP, axis=2)
    own_table = lax.dynamic_slice_in_dim(table, patch_index * C_DEV, C_DEV, axis=1)
    per_entry = jnp.where(
        incoming[0] < 0,
        0.0,
        jnp.where(incoming[0] == 0, own_table[:, 0:1], own_table[:, 1:2]),
    )
    tile_ids = jnp.arange(TILES_DEV, dtype=jnp.int32)[:, None, None]
    totals = jnp.sum(jnp.where(incoming[2][None] == tile_ids, per_entry[None], 0.0), axis=(1, 2))
    outgoing = partial.reshape(sources, TILES_DEV, R_DEV, TW)
    received = lax.all_to_all(outgoing, "visit", split_axis=0, concat_axis=0, tiled=True)
    numerator = jnp.sum(received.astype(jnp.float32), axis=0)
    coadd = (numerator / totals[:, None, None])[None]
    return (coadd, factor[None], whitened[None])


def solution(mesh):
    in_specs = (
        P(("blk", "visit"), "patch", "row", None),
        P(("blk", "visit"), "patch"),
        P(),
        P(),
        P(),
        P("blk", None),
        P(None, "blk", "patch", None),
        P(("blk", "patch"), None, ("visit", "row")),
    )
    out_specs = (
        P(("blk", "patch"), "visit", "row", None),
        P(("blk", "patch"), None, None),
        P(("blk", "patch"), None, ("visit", "row")),
    )
    return jax.shard_map(
        on_device, mesh=mesh, in_specs=in_specs, out_specs=out_specs, check_vma=False
    )
```

time: 307 us -> 61.7 us (0.20)
  matrix products: 119 us -> 3.59 us
  local copies, waits for them, and re-layouts: 79.8 us -> 6.07 us
  other arithmetic: 56.3 us -> 3.57 us
  Pallas kernels: 0 us -> 17.1 us
  waiting for transfers between devices: 21.7 us -> 9.13 us
  starting transfers between devices: 10.2 us -> 4.64 us
    dot_general x26 -> x3, matrix products: 118 us -> 3.59 us  [the longest x1 1.44 us: column_band(): out = jnp.einsum('bt,tuw->ubw', both, picks, precision=HIGHEST)]
    reshape x3 -> x2, local copies, waits for them, and re-layouts: 47.8 us -> 1.75 us  [the longest x1 1.16 us: row_band(): return out.reshape(R_DEV, BK)]
    another operation x27 -> x0, other arithmetic: 32.6 us -> none  [the longest x21 25.2 us: combine_factors(): return jnp.linalg.cholesky(joined)]
    pallas_call x0 -> x2, Pallas kernels: none -> 17.1 us  [the longest x1 10.3 us: on_device(): pl.pallas_call(window_kernel, out_shape=jax.ShapeDtypeStruct((SLABS * BK,...]
    while x5 -> x0, local copies, waits for them, and re-layouts: 13.3 us -> none  [the longest x3 12.8 us: on_device(): matched = lax.map(match_slab, (extended, row_mats))]
    all_to_all x1, waiting for transfers between devices: 21.6 us -> 9.12 us  [on_device(): lax.all_to_all(outgoing, 'visit', split_axis=0, concat_axis=0, tiled=True)]
    select_n x10 -> x4, other arithmetic: 13.2 us -> 1.15 us  [the longest x1 1.07 us: on_device(): edge = jnp.where(row_index == 0, images[:, R_DEV - HALO:], images[:, :HALO])]
    gather x2 -> x0, local copies, waits for them, and re-layouts: 6.94 us -> none  [the longest x1 6.22 us: cut_window(): return lax.dynamic_slice(matched, start, (1, out_rows, TW + 1))[0]]
  transfers between devices with their start and end apart: 3 -> 2, of which waited for: 1 -> 1; matrix products, arithmetic and copies ran while one was open for 17% -> 17% of each run, Pallas kernels for 0% -> 0%
where the time goes in v1:
time: 61.7 us; the launch traced here: 61.2 us
  Pallas kernels  17.1 us (28%)
  blocking collectives  16.3 us (26%)
  waiting for transfers between devices  9.13 us (15%)
  local copies, waits for them, and re-layouts  6.07 us (10%)
  starting transfers between devices  4.64 us (8%)
  matrix products  3.59 us (6%)
  other arithmetic  3.57 us (6%)
  between operations  0.74 us (1%)
    all_gather x1, blocking collectives, on_device(): grams = lax.all_gather(gram, ('visit', 'row'))  16.3 us
    pallas_call x1, Pallas kernels, on_device(): pl.pallas_call(window_kernel, out_shape=jax.ShapeDtypeStruct((SLABS * BK,...  10.3 us
    all_to_all x1, waiting for transfers between devices, on_device(): lax.all_to_all(outgoing, 'visit', split_axis=0, concat_axis=0, tiled=True)  9.12 us
    pallas_call x1, Pallas kernels, on_device(): pl.pallas_call(functools.partial(mix_kernel, star_total), out_shape=(jax....  6.79 us
    all_to_all x1, starting transfers between devices, on_device(): lax.all_to_all(outgoing, 'visit', split_axis=0, concat_axis=0, tiled=True)  4.12 us
    convert_element_type x2, local copies, waits for them, and re-layouts, column_band(): return out.reshape(2 * TW, NBASIS * TW).astype(jnp.bfloat16)  1.8 us
    dot_general x1, matrix products, column_band(): out = jnp.einsum('bt,tuw->ubw', both, picks, precision=HIGHEST)  1.44 us
    unnamed x7, local copies, waits for them, and re-layouts  1.29 us
  transfers between devices with their start and end apart: 2, of which 1 were waited for; matrix products, arithmetic and copies ran while one was open for 17% of the time, Pallas kernels for 0%

profile of v1, /device:TPU:0, one launch (start us, length us, event | category | flops | bytes accessed | tf_op | source)
XLA Modules:
  0.0 61.2 jit_solution(16391000292343326890)
XLA Ops:
  0.6 0.0 copy-start
  0.7 1.1 %slice_select_fusion = bf16[2,16,4096]{2,1,0:T(8,128)(2,1)S(1)} fusion(bf16[2,128,4096]{2,1,0:T(8,128)(2,1)} %bitcast.33, pred[]{:T(512)S(6)} %eq.84), kind=kLoop, calls=%fused_computation.18 | loop fusion | flops 131072 | bytes 786433 | tf_op jit(solution)/shard_map/jit(_where)/select_n | solution.py:181
  1.7 0.5 collective-permute-start
  2.3 0.7 %convert_element_type.20 = f32[4,4]{1,0:T(4,128)S(1)} convert(bf16[4,4]{1,0:T(4,128)(2,1)} %param.13) | non-fusion elementwise | flops 16 | bytes 96 | tf_op jit(solution)/shard_map/convert_element_type | solution.py:200
  3.0 0.7 %convert_element_type.21 = f32[9,21]{1,0:T(8,128)S(1)} convert(bf16[9,21]{1,0:T(8,128)(2,1)} %param.12) | non-fusion elementwise | flops 189 | bytes 1134 | tf_op jit(solution)/shard_map/convert_element_type | solution.py:32
  3.7 1.0 %fusion.27 = f32[32,32]{1,0:T(8,128)S(1)} fusion(f32[1,32,256]{2,1,0:T(8,128)} %param.15), kind=kOutput, calls=%fused_computation.48 | convolution fusion | flops 3145728 | bytes 36864 | tf_op jit(solution)/shard_map/dot_general | solution.py:178
  4.6 0.1 fusion.17
  4.7 0.7 %constant_dynamic-slice_fusion.3 = s32[3,1,1,32]{3,2,1,0:T(1,128)S(1)} fusion(s32[3,4,1,32]{3,2,1,0:T(1,128)} %param.14, s32[]{:T(128)S(6)} %select_n.69), kind=kLoop, calls=%fused_computation.46 | loop fusion | bytes 772 | tf_op jit(solution)/shard_map/jit(dynamic_index_in_dim)/dynamic_slice | solution.py:184
  5.4 0.1 constant_dynamic-slice_fusion.1
  5.5 1.4 %fusion.10 = bf16[256,9,128]{2,1,0:T(8,128)(2,1)S(1)} fusion(s32[256,128]{1,0:T(8,128)S(1)} %iota_subtract_fusion, f32[9,21]{1,0:T(8,128)S(1)} %convert_element_type.21), kind=kOutput, calls=%fused_computation.11 | convolution fusion | flops 78873168 | bytes 721652 | tf_op jit(solution)/shard_map/bt,tuw->ubw/dot_general | solution.py:40
  6.9 0.0 copy-done
  7.0 1.2 %fusion.7 = f32[128,9,144]{0,1,2:T(8,128)S(1)} fusion(f32[128]{0:T(128)S(1)} %and_select_fusion, s32[128,144]{0,1:T(8,128)S(1)} %get-tuple-element.14, s32[128,144]{0,1:T(8,128)S(1)} %get-tuple-element.13, bf16[9,21]{1,0:T(8,128)(2,1)S(1)} %copy-done), kind=kOutput, calls=%fused_computation.10 | convolution fusion | flops 43739136 | bytes 811898 | tf_op jit(solution)/shard_map/bt,tie->ibe/dot_general | solution.py:51
  8.1 0.6 dynamic-slice_bitcast_fusion.weight_ref
  8.7 0.6 copy.26
  9.3 0.7 %copy.17 = bf16[256,9,128]{0,2,1:T(8,128)(2,1)S(1)} copy(bf16[256,9,128]{2,1,0:T(8,128)(2,1)S(1)} %fusion.10) | data formatting | bytes 1179648 | tf_op jit(solution)/shard_map/convert_element_type | solution.py:41
  10.0 1.1 %copy.18.band_ref = bf16[256,1152]{1,0:T(8,128)(2,1)} copy(bf16[256,1152]{0,1:T(8,128)(2,1)S(1)} %bitcast.36) | data formatting | bytes 1179648 | tf_op jit(solution)/shard_map/convert_element_type | solution.py:41
  11.1 0.0 copy-start.2
  11.1 0.2 copy.16
  11.3 1.2 %copy.19.rows_ref = f32[128,1296]{1,0:T(8,128)} copy(f32[128,1296]{0,1:T(8,128)S(1)} %bitcast.35) | data formatting | bytes 1327104 | tf_op jit(solution)/shard_map/reshape | solution.py:52
  12.5 16.3 %all-gather = f32[256,32]{1,0:T(8,128)} all-gather(f32[32,32]{1,0:T(8,128)S(1)} %fusion.27), channel_id=2, replica_groups=mesh['blk'=2,'visit'=4,'patch'=2,'row'=2] {'visit','row'}, dimensions={0}, use_global_device_ids=true | all-gather | bytes 36864 | tf_op jit(solution)/shard_map/all_gather | solution.py:179
  28.8 0.0 copy-done.2
  28.8 0.1 broadcast_compare_fusion.1
  28.9 0.2 slice_reduce_fusion.1
  29.1 0.0 collective-permute-done.halo_ref
  29.1 0.0 copy-start.1
  29.1 0.7 %copy-done.1 = bf16[2,16,4096]{2,1,0:T(8,128)(2,1)} copy-done((bf16[2,16,4096]{2,1,0:T(8,128)(2,1)}, bf16[2,16,4096]{2,1,0:T(8,128)(2,1)S(1)}, u32[]{:S(2)}) %copy-start.1) | copy-done | bytes 262168
  29.8 10.3 %windows.1.z_ref = bf16[2592,1024]{1,0:T(8,128)(2,1)} custom-call(s32[3,32]{1,0:T(4,128)} %bitcast.40, bf16[2,128,4096]{2,1,0:T(8,128)(2,1)} %bitcast.34, bf16[2,16,4096]{2,1,0:T(8,128)(2,1)} %copy-done.1, bf16[256,1152]{1,0:T(8,128)(2,1)} %copy.18.band_ref), custom_call_target="tpu_custom_call" | custom-call | flops 2000000000 | bytes 10000000 | tf_op jit(solution)/shard_map/windows/pallas_call | solution.py:187
  40.1 6.8 %mix.1 = (bf16[8,128,128]{2,1,0:T(8,128)(2,1)}, f32[32,32]{1,0:T(8,128)}, f32[32,256]{1,0:T(8,128)}) custom-call(s32[2]{0:T(128)} %bitcast.42, f32[2]{0:T(128)} %dynamic-slice_bitcast_fusion.weight_ref, f32[8,32,32]{2,1,0:T(8,128)} %bitcast.37, f32[32,256]{1,0:T(8,128)} %bitcast.39, f32[9,16]{1,0:T(8,128)} %coeff_ref.1, f32[128,1296]{1,0:T(8,128)} %copy.19.rows_ref, ...), custom_call_target="tpu_custom_call" | custom-call | tf_op jit(solution)/shard_map/mix/pallas_call | solution.py:204
  46.9 4.1 %all-to-all-start = ((bf16[4,2,128,128]{3,2,1,0:T(8,128)(2,1)}), bf16[4,2,128,128]{3,2,1,0:T(8,128)(2,1)S(1)}, u32[]{:S(2)}, u32[]{:S(2)}) async-start(bf16[4,2,128,128]{3,2,1,0:T(8,128)(2,1)} %bitcast.38), calls=%async_computation | async-start | bytes 524288 | tf_op jit(solution)/shard_map/all_to_all | solution.py:234
  51.0 0.1 constant_dynamic-slice_fusion
  51.1 0.1 select_select_fusion
  51.2 0.1 select_reduce_fusion
  51.3 9.1 %all-to-all-done = bf16[4,2,128,128]{3,2,1,0:T(8,128)(2,1)S(1)} async-done(((bf16[4,2,128,128]{3,2,1,0:T(8,128)(2,1)}), bf16[4,2,128,128]{3,2,1,0:T(8,128)(2,1)S(1)}, u32[]{:S(2)}, u32[]{:S(2)}) %all-to-all-start) | async-done | bytes 262176 | tf_op jit(solution)/shard_map/all_to_all | solution.py:234
  60.4 0.7 %bitcast_divide_fusion = f32[1,2,128,128]{3,2,1,0:T(8,128)} fusion(f32[2,128,128]{2,1,0:T(8,128)S(1)} %convert_reduce_fusion, f32[2]{0:T(128)S(1)} %select_reduce_fusion), kind=kLoop, calls=%fused_computation.19 | loop fusion | flops 32768 | bytes 262152 | tf_op jit(solution)/shard_map/div | solution.py:236
  (4 shorter events, 0.1 us)
Async XLA Ops:
  0.6 6.3 %copy-start = (bf16[9,21]{1,0:T(8,128)(2,1)S(1)}, bf16[9,21]{1,0:T(8,128)(2,1)}, u32[]{:S(2)}) copy-start(bf16[9,21]{1,0:T(8,128)(2,1)} %param.11) | copy-start | bytes 1138
  1.7 27.3 %collective-permute-start = (bf16[2,16,4096]{2,1,0:T(8,128)(2,1)S(1)}, bf16[2,16,4096]{2,1,0:T(8,128)(2,1)S(1)}, u32[]{:S(2)}, u32[]{:S(2)}) collective-permute-start(bf16[2,16,4096]{2,1,0:T(8,128)(2,1)S(1)} %slice_select_fusion), channel_id=1, source_target_pairs={{0,1},{1,0},{2,3},{3,2},{4,5},{5,4},{6,7},{7,6},{8,9},{9,8},{10,11... | collective-permute-start | bytes 786440 | tf_op jit(solution)/shard_map/ppermute | solution.py:182
  11.1 17.7 %copy-start.2 = (s32[3,4,1,32]{3,2,1,0:T(1,128)S(1)}, s32[3,4,1,32]{3,2,1,0:T(1,128)}, u32[]{:S(2)}) copy-start(s32[3,4,1,32]{3,2,1,0:T(1,128)} %param.14) | copy-start | bytes 4612
  29.1 0.7 %copy-start.1 = (bf16[2,16,4096]{2,1,0:T(8,128)(2,1)}, bf16[2,16,4096]{2,1,0:T(8,128)(2,1)S(1)}, u32[]{:S(2)}) copy-start(bf16[2,16,4096]{2,1,0:T(8,128)(2,1)S(1)} %collective-permute-done.halo_ref) | copy-start | bytes 786436
  46.9 13.5 %all-to-all-start = ((bf16[4,2,128,128]{3,2,1,0:T(8,128)(2,1)}), bf16[4,2,128,128]{3,2,1,0:T(8,128)(2,1)S(1)}, u32[]{:S(2)}, u32[]{:S(2)}) async-start(bf16[4,2,128,128]{3,2,1,0:T(8,128)(2,1)} %bitcast.38), calls=%async_computation | async-start | bytes 524288 | tf_op jit(solution)/shard_map/all_to_all | solution.py:234

commit v2 on v1

v2 whole, which is shorter than its diff:
```python
import functools
import math

import jax
import jax.numpy as jnp
from jax import lax
from jax.experimental import pallas as pl
from jax.experimental.pallas import tpu as pltpu
from jax.sharding import PartitionSpec as P

NBASIS = 9
NTAPS = 21
C_DEV = 2
R_DEV = 128
CW = 4096
TW = 128
CAP = 8
TILES_DEV = 2
HALF = 10
SLABS = 2
HALO = 16
NCOMP = 32
PAD = 128
PAIRS = SLABS * NBASIS
OWN_K = PAIRS * R_DEV
HALO_TILES = 3
ALL_K = OWN_K + HALO_TILES * TW
HIGHEST = lax.Precision.HIGHEST
VMEM_LIMIT = 60 * 1024 * 1024
MESH = pl.DeviceIdType.MESH


def iota(shape, axis):
    return lax.broadcasted_iota(jnp.int32, shape, axis)


def window_kernel(list_ref, image_ref, sum_ref, padded, sums, sem):
    visit = lax.axis_index("visit")
    slots = list_ref.shape[3]
    loads = []
    for k in range(SLABS):
        copy = pltpu.make_async_copy(image_ref.at[0, k], padded.at[k, :, PAD : PAD + CW], sem.at[k])
        copy.start()
        loads.append(copy)
    for k in range(SLABS):
        padded[k, :, 0:PAD] = jnp.zeros((R_DEV, PAD), jnp.bfloat16)
        padded[k, :, PAD + CW :] = jnp.zeros((R_DEV, PAD), jnp.bfloat16)
    sums[...] = jnp.zeros_like(sums)
    lane = iota((R_DEV, TW), 1)
    for copy in loads:
        copy.wait()

    @pl.loop(0, slots)
    def _(q):
        k = list_ref[0, visit, 0, q]

        @pl.when(k >= 0)
        def _():
            start = list_ref[1, visit, 0, q] + (PAD - HALF)
            tile = lax.shift_right_logical(start, 7)
            shift = start - tile * TW
            back = jnp.bitwise_and(TW - shift, TW - 1)
            place = (lax.div(q, CAP) * TILES_DEV + list_ref[2, visit, 0, q]) * SLABS + k
            parts = []
            for t in range(3):
                at = pl.multiple_of((tile + t) * TW, TW)
                parts.append(pltpu.roll(padded[k, :, pl.ds(at, TW)].astype(jnp.float32), back, 1))
            keep = lane < TW - shift
            sums[place, :, 0:TW] += jnp.where(keep, parts[0], parts[1])
            sums[place, :, TW : 2 * TW] += jnp.where(keep, parts[1], parts[2])

    @pl.loop(0, sums.shape[0])
    def _(place):
        sum_ref[place] = sums[place].astype(jnp.bfloat16)


def factor_steps(gram, stars):
    sub = lax.broadcasted_iota(jnp.int32, (NCOMP, 1), 0)
    lane = lax.broadcasted_iota(jnp.int32, (NCOMP, NCOMP), 1)
    lower = jnp.zeros((NCOMP, NCOMP), jnp.float32)
    for j in range(NCOMP):
        inv = 1.0 / jnp.sqrt(gram[j : j + 1, j : j + 1])
        column = gram[:, j : j + 1] * inv
        lower = jnp.where((lane == j) & (sub >= j), column, lower)
        below = jnp.where(sub > j, column, 0.0)
        solved = stars[j : j + 1, :] * inv
        gram = gram - below * (gram[j : j + 1, :] * inv)
        stars = jnp.where(sub == j, solved, stars - below * solved)
    return lower, stars


def fused_kernel(
    visits,
    rows_count,
    star_total,
    choice_ref,
    list_vec,
    weight_ref,
    coeff_ref,
    row_tap_ref,
    column_tap_ref,
    star_ref,
    sum_ref,
    coadd_ref,
    factor_ref,
    white_ref,
    halo,
    band,
    z,
    mixed,
    grams,
    outgoing,
    incoming,
    halo_send,
    halo_recv,
    gram_send,
    gram_recv,
    tile_send,
    tile_recv,
):
    visit = lax.axis_index("visit")
    row = lax.axis_index("row")
    patch = lax.axis_index("patch")
    members = visits * rows_count
    me = visit * rows_count + row

    def member(step):
        other = lax.rem(me + step, members)
        return {"visit": lax.div(other, rows_count), "row": lax.rem(other, rows_count)}

    barrier = pltpu.get_barrier_semaphore()
    for step in range(1, members):
        pl.semaphore_signal(barrier, inc=1, device_id=member(step), device_id_type=MESH)
    stars = star_ref[0]
    grams[me] = lax.dot_general(
        stars,
        stars,
        (((1,), (1,)), ((), ())),
        precision=HIGHEST,
        preferred_element_type=jnp.float32,
    )
    pl.semaphore_wait(barrier, members - 1)
    edge = pl.multiple_of((1 - row) * (R_DEV - HALO), HALO)
    halo_copy = pltpu.make_async_remote_copy(
        src_ref=sum_ref.at[:, pl.ds(edge, HALO), :],
        dst_ref=halo,
        send_sem=halo_send,
        recv_sem=halo_recv,
        device_id={"row": 1 - row},
        device_id_type=MESH,
    )
    halo_copy.start()
    gram_copies = []
    for step in range(1, members):
        copy = pltpu.make_async_remote_copy(
            src_ref=grams.at[me],
            dst_ref=grams.at[me],
            send_sem=gram_send.at[step],
            recv_sem=gram_recv.at[step],
            device_id=member(step),
            device_id_type=MESH,
        )
        copy.start()
        gram_copies.append(copy)

    groups = visits * TILES_DEV
    z[OWN_K + PAIRS * HALO :, :] = jnp.zeros((ALL_K - OWN_K - PAIRS * HALO, groups * TW), jnp.bfloat16)
    tap = iota((NTAPS, 2 * TW), 0)
    lanes = iota((NTAPS, 2 * TW), 1)
    near = (lanes == jnp.bitwise_and(-tap, 2 * TW - 1)).astype(jnp.float32)
    far = (lanes == jnp.bitwise_and(-1 - tap, 2 * TW - 1)).astype(jnp.float32)
    reversed_taps = jnp.dot(
        column_tap_ref[...].astype(jnp.float32), 0.375 * near + 0.625 * far, precision=HIGHEST
    )
    for b in range(NBASIS):
        base = jnp.broadcast_to(reversed_taps[b : b + 1, :], (2 * TW, 2 * TW))
        rolled = pltpu.roll(base, 0, 1, stride=1, stride_axis=0)
        band[:, b * TW : (b + 1) * TW] = rolled[:, 0:TW].astype(jnp.bfloat16)

    @pl.loop(0, groups)
    def _(group):
        at = pl.ds(pl.multiple_of(group * TW, TW), TW)
        for k in range(SLABS):
            out = jnp.dot(
                sum_ref[group * SLABS + k], band[...], preferred_element_type=jnp.float32
            ).astype(jnp.bfloat16)
            for b in range(NBASIS):
                m = k * NBASIS + b
                z[m * R_DEV : (m + 1) * R_DEV, at] = out[:, b * TW : (b + 1) * TW]

    halo_copy.wait_recv()

    @pl.loop(0, groups)
    def _(group):
        at = pl.ds(pl.multiple_of(group * TW, TW), TW)
        for k in range(SLABS):
            out = jnp.dot(
                halo[group * SLABS + k], band[...], preferred_element_type=jnp.float32
            ).astype(jnp.bfloat16)
            for b in range(NBASIS):
                m = k * NBASIS + b
                z[OWN_K + m * HALO : OWN_K + (m + 1) * HALO, at] = out[:, b * TW : (b + 1) * TW]

    for copy in gram_copies:
        copy.wait_recv()
    gram = grams[0]
    for s in range(1, members):
        gram = gram + grams[s]
    lower, solved = factor_steps(gram, stars)
    root = math.sqrt(star_total)
    factor = lower / root
    factor_ref[0] = factor
    white_ref[0] = solved * root
    eye = iota((NCOMP, NCOMP), 0) == iota((NCOMP, NCOMP), 1)
    diag = jnp.sum(jnp.where(eye, factor, 0.0), axis=1, keepdims=True)[:NBASIS]
    scale = diag / jnp.sqrt(jnp.sum(diag * diag, axis=0, keepdims=True) / NBASIS)
    sets = iota(coeff_ref.shape, 1)
    table = weight_ref[...].astype(jnp.float32)
    cell_visit, cell_ccd = iota(table.shape, 0), iota(table.shape, 1)

    def weight_of(source, k):
        hit = (cell_visit == source) & (cell_ccd == patch * C_DEV + k)
        return jnp.sum(jnp.where(hit, table, 0.0), keepdims=True)

    tap = iota((NTAPS, 2 * TW), 0)
    near = (lanes == jnp.bitwise_and(tap - HALF, 2 * TW - 1)).astype(jnp.float32)
    far = (lanes == jnp.bitwise_and(tap + 1 - HALF, 2 * TW - 1)).astype(jnp.float32)
    lane = iota((R_DEV, TW), 1)
    wide_sub = iota((R_DEV, 2 * TW), 0)
    last = (wide_sub == R_DEV - 1) & (row == rows_count - 1)
    halo_parts = [jnp.zeros((R_DEV, TW), jnp.float32) for _ in range(HALO_TILES)]
    for k in range(SLABS):
        picked = jnp.sum(
            jnp.where(sets == choice_ref[0, k], coeff_ref[...], 0.0), axis=1, keepdims=True
        )
        taps = (picked * scale) * row_tap_ref[...].astype(jnp.float32)
        taps = taps.astype(jnp.bfloat16).astype(jnp.float32)
        weight = weight_of(visit, k)
        first = jnp.dot(taps, near, precision=HIGHEST) * (0.75 * weight)
        second = jnp.dot(taps, far, precision=HIGHEST) * (0.25 * weight)
        for b in range(NBASIS):
            m = k * NBASIS + b
            one = jnp.broadcast_to(first[b : b + 1], (R_DEV, 2 * TW))
            two = jnp.broadcast_to(second[b : b + 1], (R_DEV, 2 * TW))
            base = one + jnp.where(last, 0.0, two)
            rolled = pltpu.roll(base, 0, 1, stride=1, stride_axis=0)
            mixed[:, m * TW : (m + 1) * TW] = rolled[:, 0:TW].astype(jnp.bfloat16)
            low = m % 8 * HALO
            piece = pltpu.roll(rolled[:, TW:], jnp.bitwise_and(low + row * HALO, TW - 1), 1)
            inside = (lane >= low) & (lane < low + HALO)
            halo_parts[m // 8] = jnp.where(inside, piece, halo_parts[m // 8])
    for t in range(HALO_TILES):
        mixed[:, OWN_K + t * TW : OWN_K + (t + 1) * TW] = halo_parts[t].astype(jnp.bfloat16)

    tile_copies = []
    for step in range(1, visits + 1):
        owner = lax.rem(visit + step, visits)
        at = pl.ds(pl.multiple_of(owner * TILES_DEV * TW, TILES_DEV * TW), TILES_DEV * TW)
        out = jnp.dot(mixed[...], z[:, at], preferred_element_type=jnp.float32)
        out = out.astype(jnp.bfloat16)
        for g in range(TILES_DEV):
            tile = out[:, g * TW : (g + 1) * TW]
            if step < visits:
                outgoing[step, g] = tile
            else:
                incoming[visit, g] = tile
        if step < visits:
            copy = pltpu.make_async_remote_copy(
                src_ref=outgoing.at[step],
                dst_ref=incoming.at[visit],
                send_sem=tile_send.at[step],
                recv_sem=tile_recv.at[step],
                device_id={"visit": owner},
                device_id_type=MESH,
            )
            copy.start()
            tile_copies.append(copy)

    slot_lane = iota((1, list_vec.shape[3]), 1)
    mine = (slot_lane >= visit * CAP) & (slot_lane < visit * CAP + CAP)
    totals = [jnp.zeros((1, 1), jnp.float32) for _ in range(TILES_DEV)]
    for s in range(visits):
        block, slot = list_vec[0, s], list_vec[2, s]
        for g in range(TILES_DEV):
            for k in range(SLABS):
                hits = jnp.where(mine & (block == k) & (slot == g), 1.0, 0.0)
                count = jnp.sum(hits, axis=1, keepdims=True)
                totals[g] = totals[g] + count * weight_of(s, k)
    for copy in tile_copies:
        copy.wait_recv()
    for g in range(TILES_DEV):
        numerator = incoming[0, g].astype(jnp.float32)
        for s in range(1, visits):
            numerator = numerator + incoming[s, g].astype(jnp.float32)
        coadd_ref[0, g] = numerator / totals[g]
    for copy in [halo_copy] + gram_copies + tile_copies:
        copy.wait_send()


def on_device(
    exposures,
    kernel_choice,
    kernel_coeffs,
    row_taps,
    column_taps,
    visit_weight,
    footprints,
    star_coeffs,
):
    visits = lax.axis_size("visit")
    rows_count = lax.axis_size("row")
    members = visits * rows_count
    groups = visits * TILES_DEV
    star_total = star_coeffs.shape[2] * members
    vmem = pl.BlockSpec(memory_space=pltpu.VMEM)
    smem = pl.BlockSpec(memory_space=pltpu.SMEM)
    tiles = pltpu.VMEM((visits, TILES_DEV, R_DEV, TW), jnp.bfloat16)
    dma = pltpu.SemaphoreType.DMA
    sums_shape = (groups * SLABS, R_DEV, 2 * TW)
    sums = pl.pallas_call(
        window_kernel,
        out_shape=jax.ShapeDtypeStruct(sums_shape, jnp.bfloat16),
        in_specs=[smem, pl.BlockSpec(memory_space=pl.ANY)],
        out_specs=vmem,
        scratch_shapes=[
            pltpu.VMEM((SLABS, R_DEV, CW + 2 * PAD), jnp.bfloat16),
            pltpu.VMEM(sums_shape, jnp.float32),
            dma((SLABS,)),
        ],
        compiler_params=pltpu.CompilerParams(vmem_limit_bytes=VMEM_LIMIT),
        name="windows",
    )(footprints, exposures)
    return pl.pallas_call(
        functools.partial(fused_kernel, visits, rows_count, star_total),
        out_shape=(
            jax.ShapeDtypeStruct((1, TILES_DEV, R_DEV, TW), jnp.float32),
            jax.ShapeDtypeStruct((1, NCOMP, NCOMP), jnp.float32),
            jax.ShapeDtypeStruct(star_coeffs.shape, jnp.float32),
        ),
        in_specs=[smem] + [vmem] * 7,
        out_specs=(vmem, vmem, vmem),
        scratch_shapes=[
            pltpu.VMEM((groups * SLABS, HALO, 2 * TW), jnp.bfloat16),
            pltpu.VMEM((2 * TW, NBASIS * TW), jnp.bfloat16),
            pltpu.VMEM((ALL_K, groups * TW), jnp.bfloat16),
            pltpu.VMEM((R_DEV, ALL_K), jnp.bfloat16),
            pltpu.VMEM((members, NCOMP, NCOMP), jnp.float32),
            tiles,
            tiles,
            dma,
            dma,
            dma((members,)),
            dma((members,)),
            dma((visits,)),
            dma((visits,)),
        ],
        compiler_params=pltpu.CompilerParams(
            vmem_limit_bytes=VMEM_LIMIT, collective_id=0, has_side_effects=True
        ),
        name="coadd",
    )(
        kernel_choice,
        footprints,
        visit_weight,
        kernel_coeffs,
        row_taps,
        column_taps,
        star_coeffs,
        sums,
    )


def solution(mesh):
    in_specs = (
        P(("blk", "visit"), "patch", "row", None),
        P(("blk", "visit"), "patch"),
        P(),
        P(),
        P(),
        P("blk", None),
        P(None, "blk", "patch", None),
        P(("blk", "patch"), None, ("visit", "row")),
    )
    out_specs = (
        P(("blk", "patch"), "visit", "row", None),
        P(("blk", "patch"), None, None),
        P(("blk", "patch"), None, ("visit", "row")),
    )
    return jax.shard_map(
        on_device, mesh=mesh, in_specs=in_specs, out_specs=out_specs, check_vma=False
    )
```

time: 61.7 us -> 34.1 us (0.55)
  blocking collectives: 16.3 us -> 0 us
  Pallas kernels: 17.1 us -> 28.7 us
  waiting for transfers between devices: 9.13 us -> 0 us
  starting transfers between devices: 4.64 us -> 0 us
  matrix products: 3.59 us -> 0 us
  other arithmetic: 3.57 us -> 0 us
  local copies, waits for them, and re-layouts: 6.07 us -> 4.27 us
    all_gather x1 -> x0, blocking collectives: 16.3 us -> none  [on_device(): grams = lax.all_gather(gram, ('visit', 'row'))]
    pallas_call x2, Pallas kernels: 17.1 us -> 28.7 us  [the longest x1 22.8 us: on_device(): pl.pallas_call(functools.partial(fused_kernel, visits, rows_count, star_t...]
    all_to_all x1 -> x0, waiting for transfers between devices: 9.12 us -> none  [on_device(): lax.all_to_all(outgoing, 'visit', split_axis=0, concat_axis=0, tiled=True)]
    all_to_all x1 -> x0, starting transfers between devices: 4.12 us -> none  [on_device(): lax.all_to_all(outgoing, 'visit', split_axis=0, concat_axis=0, tiled=True)]
    dot_general x3 -> x0, matrix products: 3.59 us -> none  [the longest x1 1.44 us: column_band(): out = jnp.einsum('bt,tuw->ubw', both, picks, precision=HIGHEST)]
    unnamed x7 -> x3, local copies, waits for them, and re-layouts: 1.29 us -> 4.27 us
    convert_element_type x2 -> x0, local copies, waits for them, and re-layouts: 1.8 us -> none  [column_band(): return out.reshape(2 * TW, NBASIS * TW).astype(jnp.bfloat16)]
    reshape x2 -> x0, local copies, waits for them, and re-layouts: 1.75 us -> none  [the longest x1 1.16 us: row_band(): return out.reshape(R_DEV, BK)]
  transfers between devices with their start and end apart: 2 -> 0, of which waited for: 1 -> 0; matrix products, arithmetic and copies ran while one was open for 17% -> 0% of each run, Pallas kernels for 0% -> 0%
where the time goes in v2:
time: 34.1 us; the launch traced here: 33.6 us
  Pallas kernels  28.7 us (84%)
  local copies, waits for them, and re-layouts  4.27 us (13%)
  between operations  0.65 us (2%)
    pallas_call x1, Pallas kernels, on_device(): pl.pallas_call(functools.partial(fused_kernel, visits, rows_count, star_t...  22.8 us
    pallas_call x1, Pallas kernels, on_device(): pl.pallas_call(window_kernel, out_shape=jax.ShapeDtypeStruct(sums_shape,...  5.87 us
    unnamed x3, local copies, waits for them, and re-layouts  4.27 us

profile of v2, /device:TPU:0, one launch (start us, length us, event | category | flops | bytes accessed | tf_op | source)
XLA Modules:
  0.0 33.6 jit_solution(12148701143791748692)
XLA Ops:
  0.6 5.9 %windows.1.sum_ref = bf16[16,128,256]{2,1,0:T(8,128)(2,1)} custom-call(s32[3,4,1,32]{3,2,1,0:T(1,128)} %list_vec.1, bf16[1,2,128,4096]{3,2,1,0:T(8,128)(2,1)} %image_ref.1), custom_call_target="tpu_custom_call" | custom-call | tf_op jit(solution)/shard_map/windows/pallas_call | solution.py:320
  6.5 22.8 %coadd.1 = (f32[1,2,128,128]{3,2,1,0:T(8,128)}, f32[1,32,32]{2,1,0:T(8,128)}, f32[1,32,256]{2,1,0:T(8,128)}) custom-call(s32[1,2]{1,0:T(1,128)} %choice_ref.1, s32[3,4,1,32]{3,2,1,0:T(1,128)} %list_vec.1, bf16[4,4]{1,0:T(4,128)(2,1)} %weight_ref.1, f32[9,16]{1,0:T(8,128)} %coeff_ref.1, bf16[9,21]{1,0:T(8,128)(2,1)} %row_tap_ref.1, ...), custom_call_target="tpu_custom_call" | custom-call | tf_op jit(solution)/shard_map/coadd/pallas_call | solution.py:333
  29.3 1.6 %copy.14 = f32[1,2,128,128]{3,2,1,0:T(8,128)} copy(f32[1,2,128,128]{3,2,1,0:T(8,128)} %get-tuple-element.6) | data formatting | bytes 262144
  30.9 1.3 %copy.15 = f32[1,32,32]{2,1,0:T(8,128)} copy(f32[1,32,32]{2,1,0:T(8,128)} %get-tuple-element.7) | data formatting | bytes 8192
  32.2 1.4 %copy.16 = f32[1,32,256]{2,1,0:T(8,128)} copy(f32[1,32,256]{2,1,0:T(8,128)} %get-tuple-element.8) | data formatting | bytes 65536

commit v3 on v2

--- a/solution.py
+++ b/solution.py
@@ -24,6 +24,7 @@
 PAIRS = SLABS * NBASIS
 OWN_K = PAIRS * R_DEV
 HALO_TILES = 3
+BATCH = 4
 ALL_K = OWN_K + HALO_TILES * TW
 HIGHEST = lax.Precision.HIGHEST
 VMEM_LIMIT = 60 * 1024 * 1024
@@ -177,36 +178,37 @@
         rolled = pltpu.roll(base, 0, 1, stride=1, stride_axis=0)
         band[:, b * TW : (b + 1) * TW] = rolled[:, 0:TW].astype(jnp.bfloat16)
 
-    @pl.loop(0, groups)
-    def _(group):
+    def store(out, place, count, first_row):
+        group, k = place
         at = pl.ds(pl.multiple_of(group * TW, TW), TW)
-        for k in range(SLABS):
-            out = jnp.dot(
-                sum_ref[group * SLABS + k], band[...], preferred_element_type=jnp.float32
-            ).astype(jnp.bfloat16)
-            for b in range(NBASIS):
-                m = k * NBASIS + b
-                z[m * R_DEV : (m + 1) * R_DEV, at] = out[:, b * TW : (b + 1) * TW]
-
-    halo_copy.wait_recv()
-
-    @pl.loop(0, groups)
-    def _(group):
-        at = pl.ds(pl.multiple_of(group * TW, TW), TW)
-        for k in range(SLABS):
-            out = jnp.dot(
-                halo[group * SLABS + k], band[...], preferred_element_type=jnp.float32
-            ).astype(jnp.bfloat16)
-            for b in range(NBASIS):
-                m = k * NBASIS + b
-                z[OWN_K + m * HALO : OWN_K + (m + 1) * HALO, at] = out[:, b * TW : (b + 1) * TW]
+        for b in range(NBASIS):
+            z[pl.ds(first_row + (k * NBASIS + b) * count, count), at] = out[:, b * TW : (b + 1) * TW]
+
+    def filter_own(step):
+        block = sum_ref[pl.ds(step * BATCH, BATCH)].reshape(BATCH * R_DEV, 2 * TW)
+        out = jnp.dot(block, band[...], preferred_element_type=jnp.float32).astype(jnp.bfloat16)
+        for c in range(BATCH):
+            group = step * (BATCH // SLABS) + c // SLABS
+            store(out[c * R_DEV : (c + 1) * R_DEV], (group, c % SLABS), R_DEV, 0)
 
     for copy in gram_copies:
         copy.wait_recv()
+    halo_copy.wait_recv()
     gram = grams[0]
     for s in range(1, members):
         gram = gram + grams[s]
+    places = groups * SLABS
+    block = halo[...].reshape(places * HALO, 2 * TW)
+    out = jnp.dot(block, band[...], preferred_element_type=jnp.float32).astype(jnp.bfloat16)
+    for place in range(places):
+        store(out[place * HALO : (place + 1) * HALO], (place // SLABS, place % SLABS), HALO, OWN_K)
+    steps = places // BATCH
+    unrolled = min(steps, 4)
+    for step in range(unrolled):
+        filter_own(step)
     lower, solved = factor_steps(gram, stars)
+    if steps > unrolled:
+        pl.loop(unrolled, steps)(filter_own)
     root = math.sqrt(star_total)
     factor = lower / root
     factor_ref[0] = factor
@@ -295,6 +297,11 @@
         coadd_ref[0, g] = numerator / totals[g]
     for copy in [halo_copy] + gram_copies + tile_copies:
         copy.wait_send()
+
+
+def result_kernel(*refs):
+    for source, target in zip(refs[:3], refs[3:]):
+        target[...] = source[...]
 
 
 def on_device(
@@ -330,7 +337,7 @@
         compiler_params=pltpu.CompilerParams(vmem_limit_bytes=VMEM_LIMIT),
         name="windows",
     )(footprints, exposures)
-    return pl.pallas_call(
+    results = pl.pallas_call(
         functools.partial(fused_kernel, visits, rows_count, star_total),
         out_shape=(
             jax.ShapeDtypeStruct((1, TILES_DEV, R_DEV, TW), jnp.float32),
@@ -368,6 +375,13 @@
         star_coeffs,
         sums,
     )
+    return pl.pallas_call(
+        result_kernel,
+        out_shape=tuple(jax.ShapeDtypeStruct(part.shape, part.dtype) for part in results),
+        in_specs=[vmem] * 3,
+        out_specs=(vmem,) * 3,
+        name="results",
+    )(*results)
 
 
 def solution(mesh):

time: 34.1 us -> 31 us (0.909)
  local copies, waits for them, and re-layouts: 4.27 us -> 0 us
  Pallas kernels: 28.7 us -> 30.1 us
    unnamed x3 -> x0, local copies, waits for them, and re-layouts: 4.27 us -> none
    pallas_call x0 -> x1, Pallas kernels: none -> 1.59 us  [on_device(): pl.pallas_call(result_kernel, out_shape=tuple((jax.ShapeDtypeStruct(part....]
where the time goes in v3:
time: 31 us; the launch traced here: 30.8 us
  Pallas kernels  30.1 us (97%)
  between operations  0.65 us (2%)
    pallas_call x1, Pallas kernels, on_device(): pl.pallas_call(functools.partial(fused_kernel, visits, rows_count, star_t...  22.7 us
    pallas_call x1, Pallas kernels, on_device(): pl.pallas_call(window_kernel, out_shape=jax.ShapeDtypeStruct(sums_shape,...  5.79 us
    pallas_call x1, Pallas kernels, on_device(): pl.pallas_call(result_kernel, out_shape=tuple((jax.ShapeDtypeStruct(part....  1.59 us

profile of v3, /device:TPU:0, one launch (start us, length us, event | category | flops | bytes accessed | tf_op | source)
XLA Modules:
  0.0 30.8 jit_solution(8588403215654145545)
XLA Ops:
  0.6 5.8 %windows.1.sum_ref = bf16[16,128,256]{2,1,0:T(8,128)(2,1)} custom-call(s32[3,4,1,32]{3,2,1,0:T(1,128)} %list_vec.1, bf16[1,2,128,4096]{3,2,1,0:T(8,128)(2,1)} %image_ref.1), custom_call_target="tpu_custom_call" | custom-call | tf_op jit(solution)/shard_map/windows/pallas_call | solution.py:327
  6.4 22.7 %coadd.1 = (f32[1,2,128,128]{3,2,1,0:T(8,128)}, f32[1,32,32]{2,1,0:T(8,128)}, f32[1,32,256]{2,1,0:T(8,128)}) custom-call(s32[1,2]{1,0:T(1,128)} %choice_ref.1, s32[3,4,1,32]{3,2,1,0:T(1,128)} %list_vec.1, bf16[4,4]{1,0:T(4,128)(2,1)} %weight_ref.1, f32[9,16]{1,0:T(8,128)} %coeff_ref.1, bf16[9,21]{1,0:T(8,128)(2,1)} %row_tap_ref.1, ...), custom_call_target="tpu_custom_call" | custom-call | tf_op jit(solution)/shard_map/coadd/pallas_call | solution.py:340
  29.2 1.6 %results.1 = (f32[1,2,128,128]{3,2,1,0:T(8,128)}, f32[1,32,32]{2,1,0:T(8,128)}, f32[1,32,256]{2,1,0:T(8,128)}) custom-call(f32[1,2,128,128]{3,2,1,0:T(8,128)} %get-tuple-element.6.refs_0_, f32[1,32,32]{2,1,0:T(8,128)} %get-tuple-element.7.refs_1_, f32[1,32,256]{2,1,0:T(8,128)} %get-tuple-element.8.refs_2_), custom_call_target="tpu_custom_call" | custom-call | tf_op jit(solution)/shard_map/results/pallas_call | solution.py:378

commit v4 on v3

--- a/solution.py
+++ b/solution.py
@@ -80,13 +80,14 @@
     lane = lax.broadcasted_iota(jnp.int32, (NCOMP, NCOMP), 1)
     lower = jnp.zeros((NCOMP, NCOMP), jnp.float32)
     for j in range(NCOMP):
-        inv = 1.0 / jnp.sqrt(gram[j : j + 1, j : j + 1])
-        column = gram[:, j : j + 1] * inv
+        column = gram[:, j : j + 1]
+        below = jnp.where(sub > j, column / gram[j : j + 1, j : j + 1], 0.0)
         lower = jnp.where((lane == j) & (sub >= j), column, lower)
-        below = jnp.where(sub > j, column, 0.0)
-        solved = stars[j : j + 1, :] * inv
-        gram = gram - below * (gram[j : j + 1, :] * inv)
-        stars = jnp.where(sub == j, solved, stars - below * solved)
+        gram = gram - below * gram[j : j + 1, :]
+        stars = stars - below * stars[j : j + 1, :]
+    pivots = jnp.where(lane == sub, lower, 0.0)
+    lower = lower / jnp.sqrt(jnp.sum(pivots, axis=0, keepdims=True))
+    stars = stars / jnp.sqrt(jnp.sum(pivots, axis=1, keepdims=True))
     return lower, stars
 
 
@@ -166,17 +167,20 @@
 
     groups = visits * TILES_DEV
     z[OWN_K + PAIRS * HALO :, :] = jnp.zeros((ALL_K - OWN_K - PAIRS * HALO, groups * TW), jnp.bfloat16)
-    tap = iota((NTAPS, 2 * TW), 0)
-    lanes = iota((NTAPS, 2 * TW), 1)
-    near = (lanes == jnp.bitwise_and(-tap, 2 * TW - 1)).astype(jnp.float32)
-    far = (lanes == jnp.bitwise_and(-1 - tap, 2 * TW - 1)).astype(jnp.float32)
+    tap = iota((NTAPS, TW), 0)
+    lanes = iota((NTAPS, TW), 1)
+    near = (lanes == jnp.bitwise_and(-tap, TW - 1)).astype(jnp.float32)
+    far = (lanes == jnp.bitwise_and(-1 - tap, TW - 1)).astype(jnp.float32)
     reversed_taps = jnp.dot(
         column_tap_ref[...].astype(jnp.float32), 0.375 * near + 0.625 * far, precision=HIGHEST
     )
+    sub_index, lane = iota((TW, TW), 0), iota((TW, TW), 1)
     for b in range(NBASIS):
-        base = jnp.broadcast_to(reversed_taps[b : b + 1, :], (2 * TW, 2 * TW))
+        base = jnp.broadcast_to(reversed_taps[b : b + 1, :], (TW, TW))
         rolled = pltpu.roll(base, 0, 1, stride=1, stride_axis=0)
-        band[:, b * TW : (b + 1) * TW] = rolled[:, 0:TW].astype(jnp.bfloat16)
+        at = slice(b * TW, (b + 1) * TW)
+        band[0:TW, at] = jnp.where(lane <= sub_index, rolled, 0.0).astype(jnp.bfloat16)
+        band[TW : 2 * TW, at] = jnp.where(lane > sub_index, rolled, 0.0).astype(jnp.bfloat16)
 
     def store(out, place, count, first_row):
         group, k = place
@@ -224,12 +228,12 @@
         hit = (cell_visit == source) & (cell_ccd == patch * C_DEV + k)
         return jnp.sum(jnp.where(hit, table, 0.0), keepdims=True)
 
-    tap = iota((NTAPS, 2 * TW), 0)
-    near = (lanes == jnp.bitwise_and(tap - HALF, 2 * TW - 1)).astype(jnp.float32)
-    far = (lanes == jnp.bitwise_and(tap + 1 - HALF, 2 * TW - 1)).astype(jnp.float32)
-    lane = iota((R_DEV, TW), 1)
-    wide_sub = iota((R_DEV, 2 * TW), 0)
-    last = (wide_sub == R_DEV - 1) & (row == rows_count - 1)
+    near = (lanes == jnp.bitwise_and(tap - HALF, TW - 1)).astype(jnp.float32)
+    far = (lanes == jnp.bitwise_and(tap + 1 - HALF, TW - 1)).astype(jnp.float32)
+    last = (sub_index == R_DEV - 1) & (row == rows_count - 1)
+    ahead = lane - sub_index
+    own = (ahead > -TW // 2) & (ahead < TW // 2)
+    beyond = ahead * (2 * row - 1) >= TW // 2
     halo_parts = [jnp.zeros((R_DEV, TW), jnp.float32) for _ in range(HALO_TILES)]
     for k in range(SLABS):
         picked = jnp.sum(
@@ -242,13 +246,14 @@
         second = jnp.dot(taps, far, precision=HIGHEST) * (0.25 * weight)
         for b in range(NBASIS):
             m = k * NBASIS + b
-            one = jnp.broadcast_to(first[b : b + 1], (R_DEV, 2 * TW))
-            two = jnp.broadcast_to(second[b : b + 1], (R_DEV, 2 * TW))
+            one = jnp.broadcast_to(first[b : b + 1], (R_DEV, TW))
+            two = jnp.broadcast_to(second[b : b + 1], (R_DEV, TW))
             base = one + jnp.where(last, 0.0, two)
             rolled = pltpu.roll(base, 0, 1, stride=1, stride_axis=0)
-            mixed[:, m * TW : (m + 1) * TW] = rolled[:, 0:TW].astype(jnp.bfloat16)
+            mixed[:, m * TW : (m + 1) * TW] = jnp.where(own, rolled, 0.0).astype(jnp.bfloat16)
             low = m % 8 * HALO
-            piece = pltpu.roll(rolled[:, TW:], jnp.bitwise_and(low + row * HALO, TW - 1), 1)
+            piece = jnp.where(beyond, rolled, 0.0)
+            piece = pltpu.roll(piece, jnp.bitwise_and(low + row * HALO, TW - 1), 1)
             inside = (lane >= low) & (lane < low + HALO)
             halo_parts[m // 8] = jnp.where(inside, piece, halo_parts[m // 8])
     for t in range(HALO_TILES):

time: 31 us -> 31.2 us (level)
  Pallas kernels: 30.1 us -> 30.5 us
where the time goes in v4:
time: 31.2 us; the launch traced here: 31.1 us
  Pallas kernels  30.5 us (98%)
  between operations  0.65 us (2%)
    pallas_call x1, Pallas kernels, on_device(): pl.pallas_call(functools.partial(fused_kernel, visits, rows_count, star_t...  22.9 us
    pallas_call x1, Pallas kernels, on_device(): pl.pallas_call(window_kernel, out_shape=jax.ShapeDtypeStruct(sums_shape,...  5.98 us
    pallas_call x1, Pallas kernels, on_device(): pl.pallas_call(result_kernel, out_shape=tuple((jax.ShapeDtypeStruct(part....  1.59 us

profile of v4, /device:TPU:0, one launch (start us, length us, event | category | flops | bytes accessed | tf_op | source)
XLA Modules:
  0.0 31.1 jit_solution(15331772778509805777)
XLA Ops:
  0.6 6.0 %windows.1.sum_ref = bf16[16,128,256]{2,1,0:T(8,128)(2,1)} custom-call(s32[3,4,1,32]{3,2,1,0:T(1,128)} %list_vec.1, bf16[1,2,128,4096]{3,2,1,0:T(8,128)(2,1)} %image_ref.1), custom_call_target="tpu_custom_call" | custom-call | tf_op jit(solution)/shard_map/windows/pallas_call | solution.py:332
  6.6 22.9 %coadd.1 = (f32[1,2,128,128]{3,2,1,0:T(8,128)}, f32[1,32,32]{2,1,0:T(8,128)}, f32[1,32,256]{2,1,0:T(8,128)}) custom-call(s32[1,2]{1,0:T(1,128)} %choice_ref.1, s32[3,4,1,32]{3,2,1,0:T(1,128)} %list_vec.1, bf16[4,4]{1,0:T(4,128)(2,1)} %weight_ref.1, f32[9,16]{1,0:T(8,128)} %coeff_ref.1, bf16[9,21]{1,0:T(8,128)(2,1)} %row_tap_ref.1, ...), custom_call_target="tpu_custom_call" | custom-call | tf_op jit(solution)/shard_map/coadd/pallas_call | solution.py:345
  29.5 1.6 %results.1 = (f32[1,2,128,128]{3,2,1,0:T(8,128)}, f32[1,32,32]{2,1,0:T(8,128)}, f32[1,32,256]{2,1,0:T(8,128)}) custom-call(f32[1,2,128,128]{3,2,1,0:T(8,128)} %get-tuple-element.6.refs_0_, f32[1,32,32]{2,1,0:T(8,128)} %get-tuple-element.7.refs_1_, f32[1,32,256]{2,1,0:T(8,128)} %get-tuple-element.8.refs_2_), custom_call_target="tpu_custom_call" | custom-call | tf_op jit(solution)/shard_map/results/pallas_call | solution.py:383
